TPU v7x, 256 devices: a whole 4x4x8 slice. The times are simulated.
256 devices in a mesh: dp: 32 (over z, y), row: 2 (over core), col: 4 (over x).
Axes of the slice: x: 4, y: 4, z: 8, core: 2. Of those that a mesh axis runs over, the one named last changes fastest.
Arguments:
- x_input: bfloat16 [32, 32, 64, 640], P('dp', 'row', 'col'), may hold values from -6 to 6
- pre_act: bfloat16 [32, 32, 64, 640], P('dp', 'row', 'col'), may hold values from -6 to 6
- out_grad: bfloat16 [32, 32, 64, 640], P('dp', 'row', 'col'), may hold values from -0.15625 to 0.15625
- conv_weight: bfloat16 [3, 3, 640, 640], replicated, may hold values from -0.078125 to 0.078125
- q_prev: float32 [5760, 2, 64], replicated, may hold values from -6 to 6
Outputs:
- p_basis: float32 [640, 2, 64], P('dp')
- q_next: float32 [5760, 2, 64], P('dp')
All inputs are finite; a program needn't handle non-finite values.
Results may differ from a plain program's by a relative error of at most 0.0036.
Values may be sent and summed in bfloat16 or wider, within the bound.
A program may use at most 128 MiB of HBM per device.

v0:
```python
import jax
import jax.numpy as jnp
from jax import lax
from jax.sharding import PartitionSpec as P


def padded_2(value, sides, width):
    for axis, dim in sides:
        size, length = (lax.axis_size(axis), value.shape[dim])
        up = [(i, (i + 1) % size) for i in range(size - 1)]
        down = [(j, i) for i, j in up]
        last = lax.slice_in_dim(value, length - width, length, axis=dim)
        leading = lax.slice_in_dim(value, 0, width, axis=dim)
        before = lax.ppermute(last, axis, up)
        after = lax.ppermute(leading, axis, down)
        value = jnp.concatenate([before, value, after], axis=dim)
    return value


def silu_slope(pre_float):
    sigma = jax.nn.sigmoid(pre_float)
    return sigma * (1.0 + pre_float * (1.0 - sigma))


def contract_first(left, right, exact):
    if exact:
        return lax.dot_general(
            left,
            right,
            (((0,), (0,)), ((), ())),
            precision=lax.Precision.HIGHEST,
            preferred_element_type=jnp.float32,
        )
    return lax.dot_general(
        left, right, (((0,), (0,)), ((), ())), preferred_element_type=jnp.float32
    )


def tap_window(padded, shift_row, shift_col, height, breadth):
    return padded[
        1 + shift_row : 1 + shift_row + height, 1 + shift_col : 1 + shift_col + breadth, :
    ].reshape(height * breadth, padded.shape[2])


def column_terms(moments, q_prev):
    return jnp.stack(
        [contract_first(moments[layer], q_prev[:, layer, :], True) for layer in range(2)], axis=1
    )


def row_terms(moments, ortho_basis):
    return jnp.stack(
        [
            jnp.dot(
                moments[layer],
                ortho_basis[:, layer, :],
                precision=lax.Precision.HIGHEST,
                preferred_element_type=jnp.float32,
            )
            for layer in range(2)
        ],
        axis=1,
    )


def gram_of(power_raw):
    return jnp.einsum(
        "mqn,mqg->qng",
        power_raw,
        power_raw,
        precision=lax.Precision.HIGHEST,
        preferred_element_type=jnp.float32,
    )


def orthonormal(power_raw, gram_matrix):
    bases = []
    for layer in range(2):
        lower = jnp.linalg.cholesky(gram_matrix[layer])
        bases.append(
            lax.linalg.triangular_solve(
                lower, power_raw[:, layer, :], left_side=False, lower=True, transpose_a=True
            )
        )
    return jnp.stack(bases, axis=1)


def on_device(x_input, pre_act, out_grad, conv_weight, q_prev):
    height, breadth, channels = (x_input.shape[1], x_input.shape[2], x_input.shape[3])
    pixels = height * breadth
    input_tile = x_input.reshape(height, breadth, channels)
    grad_tile = out_grad.reshape(height, breadth, channels)
    pre_float = pre_act.reshape(pixels, channels).astype(jnp.float32)
    hidden_flat = jax.nn.silu(pre_float).astype(jnp.bfloat16)
    grad_pad = padded_2(grad_tile, (("row", 0), ("col", 1)), 1)
    back_grad = jnp.zeros((pixels, channels), jnp.float32)
    second_taps = []
    for shift_row in (-1, 0, 1):
        for shift_col in (-1, 0, 1):
            window = tap_window(grad_pad, -shift_row, -shift_col, height, breadth)
            back_grad = back_grad + lax.dot_general(
                window,
                conv_weight[shift_row + 1, shift_col + 1],
                (((1,), (1,)), ((), ())),
                preferred_element_type=jnp.float32,
            )
            second_taps.append(contract_first(hidden_flat, window, False))
    pre_grad = (back_grad * silu_slope(pre_float)).astype(jnp.bfloat16)
    first_taps = []
    deriv_pad = padded_2(pre_grad.reshape(height, breadth, channels), (("row", 0), ("col", 1)), 1)
    input_flat = input_tile.reshape(pixels, channels)
    for shift_row in (-1, 0, 1):
        for shift_col in (-1, 0, 1):
            first_taps.append(
                contract_first(
                    input_flat,
                    tap_window(deriv_pad, -shift_row, -shift_col, height, breadth),
                    False,
                )
            )
    moments = jnp.stack(
        [
            jnp.stack(first_taps).reshape(9 * channels, channels),
            jnp.stack(second_taps).reshape(9 * channels, channels),
        ]
    )
    kernel_rows = moments.shape[1]
    owner = lax.axis_index("dp")
    basis_count = channels // lax.axis_size("dp")
    factor_count = kernel_rows // lax.axis_size("dp")
    power_raw = lax.psum(column_terms(moments, q_prev), ("dp", "row", "col"))
    ortho_basis = orthonormal(power_raw, gram_of(power_raw))
    factor_full = lax.psum(row_terms(moments, ortho_basis), ("dp", "row", "col"))
    basis_out = lax.dynamic_slice_in_dim(ortho_basis, owner * basis_count, basis_count, 0)
    factor_out = lax.dynamic_slice_in_dim(factor_full, owner * factor_count, factor_count, 0)
    return (basis_out, factor_out)


def solution(mesh):
    placed = (
        P("dp", "row", "col", None),
        P("dp", "row", "col", None),
        P("dp", "row", "col", None),
        P(),
        P(),
    )
    return jax.shard_map(
        on_device,
        mesh=mesh,
        in_specs=placed,
        out_specs=(P("dp", None, None), P("dp", None, None)),
        check_vma=False,
    )
```

profile of v0, /device:TPU:6, one launch (start us, length us, event | category | flops | bytes accessed | tf_op | source)
XLA Modules:
  0.0 655.5 jit_solution(3594010810887087729)
XLA Ops:
  7.2 0.8 slice_bitcast_fusion.9
  8.0 1.3 collective-permute-start.1
  9.3 3.0 collective-permute-start
  12.3 1.2 fusion.43
  13.5 1.2 fusion.38
  14.7 1.1 pad_maximum_fusion.11
  15.8 1.3 collective-permute-start.3
  17.1 4.5 collective-permute-start.2
  21.7 1.1 pad_maximum_fusion.5
  22.8 1.6 fusion.23
  24.5 1.4 maximum_maximum_fusion
  26.0 0.5 bitcast_dynamic-update-slice_fusion.17
  26.5 0.5 bitcast_dynamic-update-slice_fusion.16
  26.9 0.5 bitcast_dynamic-update-slice_fusion.15
  27.4 0.5 bitcast_dynamic-update-slice_fusion.14
  27.9 0.5 bitcast_dynamic-update-slice_fusion.13
  28.5 1.1 slice-done.4
  29.6 1.1 slice-done.5
  30.7 0.5 fusion.15
  31.2 0.5 bitcast_dynamic-update-slice_fusion.12
  31.7 0.5 bitcast_dynamic-update-slice_fusion.11
  32.1 0.5 bitcast_dynamic-update-slice_fusion.10
  32.6 0.5 bitcast_dynamic-update-slice_fusion.9
  33.1 0.5 convolution_add_fusion.6
  33.6 0.5 convolution_add_fusion.5
  34.0 0.5 convolution_add_fusion.4
  34.5 0.5 convolution_add_fusion.3
  35.0 0.5 convolution_add_fusion.2
  35.4 0.5 convolution_add_fusion.1
  35.9 0.5 fusion.8
  36.4 1.4 collective-permute-start.5
  37.8 3.2 collective-permute-start.4
  41.1 8.8 %fusion.12 = f32[640,1,64]{0,2,1:T(8,128)S(1)} fusion(f32[5760,640]{1,0:T(8,128)S(1)} %bitcast.253, f32[5760,2,64]{0,2,1:T(8,128)S(1)} %copy-done.5), kind=kOutput, calls=%fused_computation.38 | convolution fusion | flops 2831155200 | bytes 16384000 | tf_op jit(solution)/shard_map/dot_general | solution.py:27
  50.0 1.3 collective-permute-start.7
  51.3 4.8 collective-permute-start.6
  56.1 1.4 collective-permute-done.6
  58.1 0.5 bitcast_dynamic-update-slice_fusion.8
  58.5 0.5 bitcast_dynamic-update-slice_fusion.7
  59.0 0.5 bitcast_dynamic-update-slice_fusion.6
  59.5 0.5 bitcast_dynamic-update-slice_fusion.5
  59.9 0.5 bitcast_dynamic-update-slice_fusion.4
  60.4 0.5 bitcast_dynamic-update-slice_fusion.3
  60.9 0.5 bitcast_dynamic-update-slice_fusion.2
  61.3 0.5 bitcast_dynamic-update-slice_fusion.1
  61.8 0.5 bitcast_dynamic-update-slice_fusion
  62.3 9.2 %fusion.9 = f32[640,1,64]{0,2,1:T(8,128)S(1)} fusion(f32[5760,640]{1,0:T(8,128)S(1)} %bitcast.249, f32[5760,2,64]{0,2,1:T(8,128)S(1)} %copy-done.5), kind=kOutput, calls=%fused_computation.37 | convolution fusion | flops 2831155200 | bytes 16384000 | tf_op jit(solution)/shard_map/dot_general | solution.py:27
  71.5 0.7 pad_maximum_fusion.7
  72.3 249.7 %all-reduce.3.cloned.1.call-done = f32[640,2,64]{0,2,1:T(8,128)} async-done(((f32[640,2,64]{0,2,1:T(8,128)}), f32[640,2,64]{0,2,1:T(8,128)}) %all-reduce.3.cloned.1.call-update) | async-done | bytes 327696 | tf_op jit(solution)/shard_map/psum | solution.py:131
  322.0 1.5 fusion.62
  323.8 5.8 cholesky.44
  329.7 0.6 compare_reduce_fusion.1
  330.3 0.7 fusion.50
  331.0 4.9 custom-call.6
  335.9 5.9 cholesky.55
  341.8 0.6 compare_reduce_fusion
  342.4 0.7 fusion.51
  343.1 4.9 custom-call.7
  348.0 1.4 fusion.45
  349.4 17.3 %convolution_bitcast_fusion = f32[5760,1,64]{0,2,1:T(8,128)S(1)} fusion(f32[5760,640]{1,0:T(8,128)} %bitcast.254, f32[64,640]{1,0:T(8,128)S(1)} %fusion.45), kind=kOutput, calls=%fused_computation | convolution fusion | flops 2831155200 | bytes 16384000 | tf_op jit(solution)/shard_map/dot_general | solution.py:54
  367.1 14.2 %convolution_bitcast_fusion.1 = f32[5760,1,64]{0,2,1:T(8,128)S(1)} fusion(f32[5760,640]{1,0:T(8,128)S(1)} %bitcast.252, f32[64,640]{1,0:T(8,128)S(1)} %fusion.46), kind=kOutput, calls=%fused_computation.1 | convolution fusion | flops 2831155200 | bytes 16384000 | tf_op jit(solution)/shard_map/dot_general | solution.py:54
  381.4 1.8 pad_maximum_fusion
  383.3 0.7 copy.11
  384.0 262.8 %all-reduce.5.cloned.1.call-done = f32[5760,2,64]{0,2,1:T(8,128)} async-done(((f32[5760,2,64]{0,2,1:T(8,128)}), f32[5760,2,64]{0,2,1:T(8,128)}) %all-reduce.5.cloned.1.call-update) | async-done | bytes 2949136 | tf_op jit(solution)/shard_map/psum | solution.py:133
  646.8 1.7 constant_dynamic-slice_fusion
  (52 shorter events, 1.7 us)
Async XLA Ops:
  7.2 50.9 %copy-start = (bf16[1,16,16,640]{3,2,1,0:T(8,128)(2,1)S(1)}, bf16[1,16,16,640]{3,2,1,0:T(8,128)(2,1)}, u32[]{:S(2)}) copy-start(bf16[1,16,16,640]{3,2,1,0:T(8,128)(2,1)} %param.8) | copy-start | bytes 983044
  7.2 314.9 %all-reduce.3.cloned.1.call-start = ((), (), s32[]{:S(2)}) async-start(), calls=%async_computation | async-start | bytes 655360 | tf_op jit(solution)/shard_map/psum | solution.py:131
  8.0 6.7 %collective-permute-start.1 = (bf16[1,16,640]{2,1,0:T(8,128)(2,1)S(1)}, bf16[1,16,640]{2,1,0:T(8,128)(2,1)S(1)}, u32[]{:S(2)}, u32[]{:S(2)}) collective-permute-start(bf16[1,16,640]{2,1,0:T(8,128)(2,1)S(1)} %get-tuple-element.33), channel_id=1, source_target_pairs={{4,0},{5,1},{6,2},{7,3},{12,8},{13,9},{14,10},{15,11},{20,16},{21,... | collective-permute-start | bytes 61448 | tf_op jit(solution)/shard_map/ppermute | solution.py:15
  9.3 5.4 collective-permute-start
  15.8 8.6 %collective-permute-start.3 = (bf16[18,1,640]{2,1,0:T(2,128)(2,1)S(1)}, bf16[18,1,640]{2,1,0:T(2,128)(2,1)S(1)}, u32[]{:S(2)}, u32[]{:S(2)}) collective-permute-start(bf16[18,1,640]{2,1,0:T(2,128)(2,1)S(1)} %get-tuple-element.24), channel_id=1, source_target_pairs={{0,1},{1,2},{2,3},{4,5},{5,6},{6,7},{8,9},{9,10},{10,11},{12,13},{... | collective-permute-start | bytes 69128 | tf_op jit(solution)/shard_map/ppermute | solution.py:14
  17.1 7.3 %collective-permute-start.2 = (bf16[18,1,640]{2,1,0:T(2,128)(2,1)S(1)}, bf16[18,1,640]{2,1,0:T(2,128)(2,1)S(1)}, u32[]{:S(2)}, u32[]{:S(2)}) collective-permute-start(bf16[18,1,640]{2,1,0:T(2,128)(2,1)S(1)} %get-tuple-element.25), channel_id=1, source_target_pairs={{1,0},{2,1},{3,2},{5,4},{6,5},{7,6},{9,8},{10,9},{11,10},{13,12},{... | collective-permute-start | bytes 69128 | tf_op jit(solution)/shard_map/ppermute | solution.py:15
  24.4 3.5 copy-start.3
  24.4 3.5 copy-start.6
  27.4 2.2 slice-start.4
  27.9 2.8 slice-start.5
  33.1 8.0 %copy-start.2 = (f32[9,640,640]{2,1,0:T(8,128)}, f32[9,640,640]{2,1,0:T(8,128)S(1)}, u32[]{:S(2)}) copy-start(f32[9,640,640]{2,1,0:T(8,128)S(1)} %bitcast_dynamic-update-slice_fusion.9) | copy-start | bytes 44236804
  33.5 7.5 %copy-start.5 = (f32[5760,2,64]{0,2,1:T(8,128)S(1)}, f32[5760,2,64]{0,2,1:T(8,128)}, u32[]{:S(2)}) copy-start(f32[5760,2,64]{0,2,1:T(8,128)} %param.12) | copy-start | bytes 8847364
  36.4 13.5 %collective-permute-start.5 = (bf16[1,16,640]{2,1,0:T(8,128)(2,1)S(1)}, bf16[1,16,640]{2,1,0:T(8,128)(2,1)S(1)}, u32[]{:S(2)}, u32[]{:S(2)}) collective-permute-start(bf16[1,16,640]{2,1,0:T(8,128)(2,1)S(1)} %get-tuple-element.29), channel_id=1, source_target_pairs={{4,0},{5,1},{6,2},{7,3},{12,8},{13,9},{14,10},{15,11},{20,16},{21,... | collective-permute-start | bytes 61448 | tf_op jit(solution)/shard_map/ppermute | solution.py:15
  37.8 12.1 %collective-permute-start.4 = (bf16[1,16,640]{2,1,0:T(8,128)(2,1)S(1)}, bf16[1,16,640]{2,1,0:T(8,128)(2,1)S(1)}, u32[]{:S(2)}, u32[]{:S(2)}) collective-permute-start(bf16[1,16,640]{2,1,0:T(8,128)(2,1)S(1)} %get-tuple-element.28), channel_id=1, source_target_pairs={{0,4},{1,5},{2,6},{3,7},{8,12},{9,13},{10,14},{11,15},{16,20},{17,... | collective-permute-start | bytes 61448 | tf_op jit(solution)/shard_map/ppermute | solution.py:14
  50.0 6.1 collective-permute-start.7
  51.3 6.3 collective-permute-start.6
  62.3 9.3 %copy-start.1 = (f32[9,640,640]{2,1,0:T(8,128)}, f32[9,640,640]{2,1,0:T(8,128)S(1)}, u32[]{:S(2)}) copy-start(f32[9,640,640]{2,1,0:T(8,128)S(1)} %bitcast_dynamic-update-slice_fusion) | copy-start | bytes 44236804
  72.3 574.5 %all-reduce.5.cloned.1.call-start = ((), (), s32[]{:S(2)}) async-start(), calls=%async_computation.1 | async-start | bytes 5898240 | tf_op jit(solution)/shard_map/psum | solution.py:133
  348.0 19.1 %slice-start = ((s8[14745600]{0:T(1024)(128)(4,1)}), s8[4194304]{0:T(1024)(128)(4,1)S(1)}, s32[]{:S(2)}) async-start(s8[14745600]{0:T(1024)(128)(4,1)} %bitcast.250), calls=%async_computation.2 | async-start | bytes 8388608
  349.4 17.3 %copy-start.4 = (f32[640,2,64]{0,2,1:T(8,128)S(1)}, f32[640,2,64]{0,2,1:T(8,128)}, u32[]{:S(2)}) copy-start(f32[640,2,64]{0,2,1:T(8,128)} %all-reduce.3.cloned.1.call-done) | copy-start | bytes 983044
  349.4 17.7 %slice-start.1 = ((s8[14745600]{0:T(1024)(128)(4,1)}), s8[4194304]{0:T(1024)(128)(4,1)S(1)}, s32[]{:S(2)}) async-start(s8[14745600]{0:T(1024)(128)(4,1)} %bitcast.250), calls=%async_computation.3 | async-start | bytes 8388608
  349.4 17.7 %slice-start.2 = ((s8[14745600]{0:T(1024)(128)(4,1)}), s8[4194304]{0:T(1024)(128)(4,1)S(1)}, s32[]{:S(2)}) async-start(s8[14745600]{0:T(1024)(128)(4,1)} %bitcast.250), calls=%async_computation.4 | async-start | bytes 8388608
  349.4 17.7 %slice-start.3 = ((s8[14745600]{0:T(1024)(128)(4,1)}), s8[2162688]{0:T(1024)(128)(4,1)S(1)}, s32[]{:S(2)}) async-start(s8[14745600]{0:T(1024)(128)(4,1)} %bitcast.250), calls=%async_computation.5 | async-start | bytes 4325376
Sparse Core Ops, SparseCore 0:
  72.4 249.5 all-reduce.2
  383.3 263.3 all-reduce.4
where the time goes:
time: 662 us; the launch traced here: 655 us
  waiting for transfers between devices  514 us (78%)
  matrix products  66.6 us (10%)
  other arithmetic  33.2 us (5%)
  starting transfers between devices  20.9 us (3%)
  between operations  14.8 us (2%)
    psum x1, waiting for transfers between devices, on_device(): lax.psum(row_terms(moments, ortho_basis), ('dp', 'row', 'col'))  263 us
    psum x1, waiting for transfers between devices, on_device(): power_raw = lax.psum(column_terms(moments, q_prev), ('dp', 'row', 'col'))  250 us
    dot_general x2, matrix products, row_terms(): jnp.dot(moments[layer], ortho_basis[:, layer, :], precision=lax.Precision...  31.5 us
    dot_general x2, matrix products, contract_first(): lax.dot_general(left, right, (((0,), (0,)), ((), ())), precision=lax.Prec...  18.1 us
  transfers between devices with their start and end apart: 10, of which 3 were waited for; matrix products, arithmetic and copies ran while one was open for 2% of the time, Pallas kernels for 0%

commit v1 on v0

--- a/solution.py
+++ b/solution.py
@@ -130,7 +130,7 @@
     factor_count = kernel_rows // lax.axis_size("dp")
     power_raw = lax.psum(column_terms(moments, q_prev), ("dp", "row", "col"))
     ortho_basis = orthonormal(power_raw, gram_of(power_raw))
-    factor_full = lax.psum(row_terms(moments, ortho_basis), ("dp", "row", "col"))
+    factor_full = lax.psum(lax.psum(row_terms(moments, ortho_basis), "dp"), ("row", "col"))
     basis_out = lax.dynamic_slice_in_dim(ortho_basis, owner * basis_count, basis_count, 0)
     factor_out = lax.dynamic_slice_in_dim(factor_full, owner * factor_count, factor_count, 0)
     return (basis_out, factor_out)

time: 662 us -> 627 us (0.947)
  waiting for transfers between devices: 514 us -> 477 us
    psum x1 -> x2, waiting for transfers between devices: 263 us -> 226 us  [the longest x1 156 us: on_device(): lax.psum(row_terms(moments, ortho_basis), 'dp')]
  transfers between devices with their start and end apart: 10 -> 11, of which waited for: 3 -> 4; matrix products, arithmetic and copies ran while one was open for 2% -> 2% of each run, Pallas kernels for 0% -> 0%
where the time goes in v1:
time: 627 us; the launch traced here: 618 us
  waiting for transfers between devices  477 us (76%)
  matrix products  66.6 us (11%)
  other arithmetic  33.2 us (5%)
  starting transfers between devices  20.9 us (3%)
  between operations  14.5 us (2%)
    psum x1, waiting for transfers between devices, on_device(): power_raw = lax.psum(column_terms(moments, q_prev), ('dp', 'row', 'col'))  250 us
    psum x1, waiting for transfers between devices, on_device(): lax.psum(row_terms(moments, ortho_basis), 'dp')  156 us
    psum x1, waiting for transfers between devices, on_device(): lax.psum(lax.psum(row_terms(moments, ortho_basis), 'dp'), ('row', 'col'))  69.8 us
    dot_general x2, matrix products, row_terms(): jnp.dot(moments[layer], ortho_basis[:, layer, :], precision=lax.Precision...  31.5 us
    dot_general x2, matrix products, contract_first(): lax.dot_general(left, right, (((0,), (0,)), ((), ())), precision=lax.Prec...  18.1 us
    another operation x6, other arithmetic, orthonormal(): lower = jnp.linalg.cholesky(gram_matrix[layer])  13.1 us
  transfers between devices with their start and end apart: 11, of which 4 were waited for; matrix products, arithmetic and copies ran while one was open for 2% of the time, Pallas kernels for 0%

profile of v1, /device:TPU:6, one launch (start us, length us, event | category | flops | bytes accessed | tf_op | source)
XLA Modules:
  0.0 618.1 jit_solution(10164900037713593646)
XLA Ops:
  7.2 0.8 slice_bitcast_fusion.9
  8.0 1.3 collective-permute-start.1
  9.3 3.0 collective-permute-start
  12.3 1.2 fusion.43
  13.5 1.2 fusion.38
  14.7 1.1 pad_maximum_fusion.11
  15.8 1.3 collective-permute-start.3
  17.1 4.5 collective-permute-start.2
  21.7 1.1 pad_maximum_fusion.5
  22.8 1.6 fusion.23
  24.5 1.4 maximum_maximum_fusion
  26.0 0.5 bitcast_dynamic-update-slice_fusion.17
  26.5 0.5 bitcast_dynamic-update-slice_fusion.16
  26.9 0.5 bitcast_dynamic-update-slice_fusion.15
  27.4 0.5 bitcast_dynamic-update-slice_fusion.14
  27.9 0.5 bitcast_dynamic-update-slice_fusion.13
  28.5 1.1 slice-done.4
  29.6 1.1 slice-done.5
  30.7 0.5 fusion.15
  31.2 0.5 bitcast_dynamic-update-slice_fusion.12
  31.7 0.5 bitcast_dynamic-update-slice_fusion.11
  32.1 0.5 bitcast_dynamic-update-slice_fusion.10
  32.6 0.5 bitcast_dynamic-update-slice_fusion.9
  33.1 0.5 convolution_add_fusion.6
  33.6 0.5 convolution_add_fusion.5
  34.5 0.5 convolution_add_fusion.3
  35.0 0.5 convolution_add_fusion.2
  35.4 0.5 convolution_add_fusion.1
  35.9 0.5 fusion.8
  36.4 1.4 collective-permute-start.5
  37.8 3.2 collective-permute-start.4
  41.1 8.8 %fusion.12 = f32[640,1,64]{0,2,1:T(8,128)S(1)} fusion(f32[5760,640]{1,0:T(8,128)S(1)} %bitcast.253, f32[5760,2,64]{0,2,1:T(8,128)S(1)} %copy-done.5), kind=kOutput, calls=%fused_computation.38 | convolution fusion | flops 2831155200 | bytes 16384000 | tf_op jit(solution)/shard_map/dot_general | solution.py:27
  50.0 1.3 collective-permute-start.7
  51.3 4.8 collective-permute-start.6
  56.1 1.4 collective-permute-done.6
  58.1 0.5 bitcast_dynamic-update-slice_fusion.8
  58.5 0.5 bitcast_dynamic-update-slice_fusion.7
  59.0 0.5 bitcast_dynamic-update-slice_fusion.6
  59.5 0.5 bitcast_dynamic-update-slice_fusion.5
  59.9 0.5 bitcast_dynamic-update-slice_fusion.4
  60.4 0.5 bitcast_dynamic-update-slice_fusion.3
  60.9 0.5 bitcast_dynamic-update-slice_fusion.2
  61.3 0.5 bitcast_dynamic-update-slice_fusion.1
  61.8 0.5 bitcast_dynamic-update-slice_fusion
  62.3 9.2 %fusion.9 = f32[640,1,64]{0,2,1:T(8,128)S(1)} fusion(f32[5760,640]{1,0:T(8,128)S(1)} %bitcast.249, f32[5760,2,64]{0,2,1:T(8,128)S(1)} %copy-done.5), kind=kOutput, calls=%fused_computation.37 | convolution fusion | flops 2831155200 | bytes 16384000 | tf_op jit(solution)/shard_map/dot_general | solution.py:27
  71.5 0.7 pad_maximum_fusion.7
  72.3 249.7 %all-reduce.4.cloned.1.call-done = f32[640,2,64]{0,2,1:T(8,128)} async-done(((f32[640,2,64]{0,2,1:T(8,128)}), f32[640,2,64]{0,2,1:T(8,128)}) %all-reduce.4.cloned.1.call-update) | async-done | bytes 327696 | tf_op jit(solution)/shard_map/psum | solution.py:131
  322.0 1.5 fusion.62
  323.8 5.8 cholesky.44
  329.7 0.6 compare_reduce_fusion.1
  330.3 0.7 fusion.50
  331.0 4.9 custom-call.6
  335.9 5.9 cholesky.55
  341.8 0.6 compare_reduce_fusion
  342.4 0.7 fusion.51
  343.1 4.9 custom-call.7
  348.0 1.4 fusion.45
  349.4 17.3 %convolution_bitcast_fusion = f32[5760,1,64]{0,2,1:T(8,128)S(1)} fusion(f32[5760,640]{1,0:T(8,128)} %bitcast.254, f32[64,640]{1,0:T(8,128)S(1)} %fusion.45), kind=kOutput, calls=%fused_computation | convolution fusion | flops 2831155200 | bytes 16384000 | tf_op jit(solution)/shard_map/dot_general | solution.py:54
  367.1 14.2 %convolution_bitcast_fusion.1 = f32[5760,1,64]{0,2,1:T(8,128)S(1)} fusion(f32[5760,640]{1,0:T(8,128)S(1)} %bitcast.252, f32[64,640]{1,0:T(8,128)S(1)} %fusion.46), kind=kOutput, calls=%fused_computation.1 | convolution fusion | flops 2831155200 | bytes 16384000 | tf_op jit(solution)/shard_map/dot_general | solution.py:54
  381.4 1.8 pad_maximum_fusion
  383.2 155.9 %all-reduce.6.cloned.1.call-done = f32[5760,2,64]{0,2,1:T(8,128)} async-done(((f32[5760,2,64]{0,2,1:T(8,128)}), f32[5760,2,64]{0,2,1:T(8,128)}) %all-reduce.6.cloned.1.call-update) | async-done | bytes 2949136 | tf_op jit(solution)/shard_map/psum | solution.py:133
  539.2 0.7 copy.11
  539.9 69.8 %all-reduce.8.cloned.1.call-done = f32[5760,2,64]{0,2,1:T(8,128)} async-done(((f32[5760,2,64]{0,2,1:T(8,128)}), f32[5760,2,64]{0,2,1:T(8,128)}) %all-reduce.8.cloned.1.call-update) | async-done | bytes 2949136 | tf_op jit(solution)/shard_map/psum | solution.py:133
  609.7 1.7 constant_dynamic-slice_fusion
  (55 shorter events, 2.2 us)
Async XLA Ops:
  7.2 50.9 %copy-start = (bf16[1,16,16,640]{3,2,1,0:T(8,128)(2,1)S(1)}, bf16[1,16,16,640]{3,2,1,0:T(8,128)(2,1)}, u32[]{:S(2)}) copy-start(bf16[1,16,16,640]{3,2,1,0:T(8,128)(2,1)} %param.8) | copy-start | bytes 983044
  7.2 314.9 %all-reduce.4.cloned.1.call-start = ((), (), s32[]{:S(2)}) async-start(), calls=%async_computation | async-start | bytes 655360 | tf_op jit(solution)/shard_map/psum | solution.py:131
  8.0 6.7 %collective-permute-start.1 = (bf16[1,16,640]{2,1,0:T(8,128)(2,1)S(1)}, bf16[1,16,640]{2,1,0:T(8,128)(2,1)S(1)}, u32[]{:S(2)}, u32[]{:S(2)}) collective-permute-start(bf16[1,16,640]{2,1,0:T(8,128)(2,1)S(1)} %get-tuple-element.33), channel_id=1, source_target_pairs={{4,0},{5,1},{6,2},{7,3},{12,8},{13,9},{14,10},{15,11},{20,16},{21,... | collective-permute-start | bytes 61448 | tf_op jit(solution)/shard_map/ppermute | solution.py:15
  9.3 5.4 collective-permute-start
  15.8 8.6 %collective-permute-start.3 = (bf16[18,1,640]{2,1,0:T(2,128)(2,1)S(1)}, bf16[18,1,640]{2,1,0:T(2,128)(2,1)S(1)}, u32[]{:S(2)}, u32[]{:S(2)}) collective-permute-start(bf16[18,1,640]{2,1,0:T(2,128)(2,1)S(1)} %get-tuple-element.24), channel_id=1, source_target_pairs={{0,1},{1,2},{2,3},{4,5},{5,6},{6,7},{8,9},{9,10},{10,11},{12,13},{... | collective-permute-start | bytes 69128 | tf_op jit(solution)/shard_map/ppermute | solution.py:14
  17.1 7.3 %collective-permute-start.2 = (bf16[18,1,640]{2,1,0:T(2,128)(2,1)S(1)}, bf16[18,1,640]{2,1,0:T(2,128)(2,1)S(1)}, u32[]{:S(2)}, u32[]{:S(2)}) collective-permute-start(bf16[18,1,640]{2,1,0:T(2,128)(2,1)S(1)} %get-tuple-element.25), channel_id=1, source_target_pairs={{1,0},{2,1},{3,2},{5,4},{6,5},{7,6},{9,8},{10,9},{11,10},{13,12},{... | collective-permute-start | bytes 69128 | tf_op jit(solution)/shard_map/ppermute | solution.py:15
  24.4 3.5 copy-start.3
  24.4 3.5 copy-start.6
  27.4 2.2 slice-start.4
  27.9 2.8 slice-start.5
  33.1 8.0 %copy-start.2 = (f32[9,640,640]{2,1,0:T(8,128)}, f32[9,640,640]{2,1,0:T(8,128)S(1)}, u32[]{:S(2)}) copy-start(f32[9,640,640]{2,1,0:T(8,128)S(1)} %bitcast_dynamic-update-slice_fusion.9) | copy-start | bytes 44236804
  33.5 7.5 %copy-start.5 = (f32[5760,2,64]{0,2,1:T(8,128)S(1)}, f32[5760,2,64]{0,2,1:T(8,128)}, u32[]{:S(2)}) copy-start(f32[5760,2,64]{0,2,1:T(8,128)} %param.12) | copy-start | bytes 8847364
  36.4 13.5 %collective-permute-start.5 = (bf16[1,16,640]{2,1,0:T(8,128)(2,1)S(1)}, bf16[1,16,640]{2,1,0:T(8,128)(2,1)S(1)}, u32[]{:S(2)}, u32[]{:S(2)}) collective-permute-start(bf16[1,16,640]{2,1,0:T(8,128)(2,1)S(1)} %get-tuple-element.29), channel_id=1, source_target_pairs={{4,0},{5,1},{6,2},{7,3},{12,8},{13,9},{14,10},{15,11},{20,16},{21,... | collective-permute-start | bytes 61448 | tf_op jit(solution)/shard_map/ppermute | solution.py:15
  37.8 12.1 %collective-permute-start.4 = (bf16[1,16,640]{2,1,0:T(8,128)(2,1)S(1)}, bf16[1,16,640]{2,1,0:T(8,128)(2,1)S(1)}, u32[]{:S(2)}, u32[]{:S(2)}) collective-permute-start(bf16[1,16,640]{2,1,0:T(8,128)(2,1)S(1)} %get-tuple-element.28), channel_id=1, source_target_pairs={{0,4},{1,5},{2,6},{3,7},{8,12},{9,13},{10,14},{11,15},{16,20},{17,... | collective-permute-start | bytes 61448 | tf_op jit(solution)/shard_map/ppermute | solution.py:14
  50.0 6.1 collective-permute-start.7
  51.3 6.3 %collective-permute-start.6 = (bf16[18,1,640]{2,1,0:T(2,128)(2,1)S(1)}, bf16[18,1,640]{2,1,0:T(2,128)(2,1)S(1)}, u32[]{:S(2)}, u32[]{:S(2)}) collective-permute-start(bf16[18,1,640]{2,1,0:T(2,128)(2,1)S(1)} %get-tuple-element.21), channel_id=1, source_target_pairs={{1,0},{2,1},{3,2},{5,4},{6,5},{7,6},{9,8},{10,9},{11,10},{13,12},{... | collective-permute-start | bytes 69128 | tf_op jit(solution)/shard_map/ppermute | solution.py:15
  62.3 9.3 %copy-start.1 = (f32[9,640,640]{2,1,0:T(8,128)}, f32[9,640,640]{2,1,0:T(8,128)S(1)}, u32[]{:S(2)}) copy-start(f32[9,640,640]{2,1,0:T(8,128)S(1)} %bitcast_dynamic-update-slice_fusion) | copy-start | bytes 44236804
  72.3 466.8 %all-reduce.6.cloned.1.call-start = ((), (), s32[]{:S(2)}) async-start(), calls=%async_computation.1 | async-start | bytes 5898240 | tf_op jit(solution)/shard_map/psum | solution.py:133
  348.0 19.1 %slice-start = ((s8[14745600]{0:T(1024)(128)(4,1)}), s8[4194304]{0:T(1024)(128)(4,1)S(1)}, s32[]{:S(2)}) async-start(s8[14745600]{0:T(1024)(128)(4,1)} %bitcast.250), calls=%async_computation.3 | async-start | bytes 8388608
  349.4 17.3 %copy-start.4 = (f32[640,2,64]{0,2,1:T(8,128)S(1)}, f32[640,2,64]{0,2,1:T(8,128)}, u32[]{:S(2)}) copy-start(f32[640,2,64]{0,2,1:T(8,128)} %all-reduce.4.cloned.1.call-done) | copy-start | bytes 983044
  349.4 17.7 %slice-start.1 = ((s8[14745600]{0:T(1024)(128)(4,1)}), s8[4194304]{0:T(1024)(128)(4,1)S(1)}, s32[]{:S(2)}) async-start(s8[14745600]{0:T(1024)(128)(4,1)} %bitcast.250), calls=%async_computation.4 | async-start | bytes 8388608
  349.4 17.7 %slice-start.2 = ((s8[14745600]{0:T(1024)(128)(4,1)}), s8[4194304]{0:T(1024)(128)(4,1)S(1)}, s32[]{:S(2)}) async-start(s8[14745600]{0:T(1024)(128)(4,1)} %bitcast.250), calls=%async_computation.5 | async-start | bytes 8388608
  349.4 17.7 %slice-start.3 = ((s8[14745600]{0:T(1024)(128)(4,1)}), s8[2162688]{0:T(1024)(128)(4,1)S(1)}, s32[]{:S(2)}) async-start(s8[14745600]{0:T(1024)(128)(4,1)} %bitcast.250), calls=%async_computation.6 | async-start | bytes 4325376
  383.2 226.5 %all-reduce.8.cloned.1.call-start = ((), (), s32[]{:S(2)}) async-start(), calls=%async_computation.2 | async-start | bytes 5898240 | tf_op jit(solution)/shard_map/psum | solution.py:133
Sparse Core Ops, SparseCore 0:
  72.4 249.5 all-reduce.3
  383.3 155.7 all-reduce.5
  541.6 68.0 all-reduce.7
